TPU v7x, 128 devices: a whole 4x4x4 slice. The times are simulated.
128 devices in a mesh: grp: 4 (over z), exp: 8 (over x, core), ten: 4 (over y).
Axes of the slice: x: 4, y: 4, z: 4, core: 2. Of those that a mesh axis runs over, the one named last changes fastest.
Arguments:
- tokens: bfloat16 [4096, 4096], P(('grp', 'exp', 'ten')), parts along dimension 0, may hold values from -100 to 100
- norm_gain: float32 [4096], replicated, may hold values from 0.1 to 1.9
- expert_ids: int32 [4096, 8], P(('grp', 'exp', 'ten')), parts along dimension 0, may hold values from 0 to 15, as said below
- gate_prob: float32 [4096, 8], P(('grp', 'exp', 'ten')), parts along dimension 0, may hold values from 0.05 to 1
- w_gate: bfloat16 [16, 4096, 1536], P('exp', None, 'ten'), may hold values from -0.09375 to 0.09375
- w_up: bfloat16 [16, 4096, 1536], P('exp', None, 'ten'), may hold values from -0.09375 to 0.09375
- w_down: bfloat16 [16, 1536, 4096], P('exp', 'ten'), may hold values from -0.15625 to 0.15625
Outputs:
- mixed: bfloat16 [4096, 4096], P(('grp', 'exp', 'ten')), parts along dimension 0
There are 4 independent parts, one for each index of `grp`. A program takes and returns all parts, laid end to end along the dimension named above; an argument that names none is the same for every part. Nothing has to cross between parts.
Inputs may be any that keep to these rules, and one draw needn't show every extreme that they name: `expert_ids`: each row names 8 different experts. Within the rows of one device no expert is named by more than 24 rows, and in every draw one expert is named by exactly 24 rows of every device.
All inputs are finite; a program needn't handle non-finite values.
Results may differ from a plain program's by a relative error of at most 0.012.
Values may be sent and summed in bfloat16 or wider, within the bound.
A program may use at most 128 MiB of HBM per device.

v0:
```python
import jax
import jax.numpy as jnp
from jax import lax
from jax.sharding import PartitionSpec as P


def expert_pass(piece, w_gate, w_up, w_down):
    gate_part = jnp.einsum("abecd,edf->abecf", piece, w_gate, preferred_element_type=jnp.float32)
    up_part = jnp.einsum("abecd,edf->abecf", piece, w_up, preferred_element_type=jnp.float32)
    hidden = (jax.nn.silu(gate_part) * up_part).astype(jnp.bfloat16)
    return jnp.einsum("abecf,efd->abecd", hidden, w_down, preferred_element_type=jnp.float32)


def per_device(tokens, norm_gain, expert_ids, gate_prob, w_gate, w_up, w_down):
    tok_rows, width = tokens.shape
    top_count = expert_ids.shape[1]
    exp_count = lax.axis_size("exp")
    ten_count = lax.axis_size("ten")
    local_count = w_gate.shape[0]
    expert_count = local_count * exp_count
    capacity = 3 * tok_rows // 4
    floats = tokens.astype(jnp.float32)
    meansq = jnp.mean(floats * floats, axis=1, keepdims=True)
    normed = (floats * lax.rsqrt(meansq + 1e-06) * norm_gain).astype(jnp.bfloat16)
    mixing = gate_prob / jnp.sum(gate_prob, axis=1, keepdims=True)
    flat_ids = expert_ids.reshape(-1)
    member = (flat_ids[:, None] == jnp.arange(expert_count, dtype=jnp.int32)[None, :]).astype(
        jnp.int32
    )
    earlier = jnp.cumsum(member, axis=0) - member
    slot_index = jnp.sum(earlier * member, axis=1)
    target = flat_ids * capacity + slot_index
    placing = jnp.arange(expert_count * capacity, dtype=jnp.int32)[:, None] == target[None, :]
    placing = jnp.any(placing.reshape(expert_count * capacity, tok_rows, top_count), axis=2).astype(
        jnp.bfloat16
    )
    outgoing = jnp.dot(placing, normed, preferred_element_type=jnp.float32).astype(jnp.bfloat16)
    outgoing = outgoing.reshape(exp_count, local_count, capacity, width)
    arrived = lax.all_to_all(outgoing, "exp", split_axis=0, concat_axis=0, tiled=True)
    arrived = arrived.reshape(exp_count, 1, local_count, capacity, width)
    partial_value = expert_pass(
        lax.all_gather(arrived, "ten", axis=1, tiled=True), w_gate, w_up, w_down
    )
    sendback = partial_value.astype(jnp.bfloat16).reshape(
        exp_count * ten_count, local_count * capacity, width
    )
    returned = lax.all_to_all(sendback, ("exp", "ten"), split_axis=0, concat_axis=0, tiled=True)
    returned = returned.reshape(exp_count, ten_count, local_count * capacity, width)
    combined = jnp.sum(returned, axis=1, dtype=jnp.float32).astype(jnp.bfloat16)
    combined = combined.reshape(expert_count * capacity, width)
    picked = jnp.take(combined, target, axis=0).reshape(tok_rows, top_count, width)
    mixed = jnp.sum(mixing[:, :, None] * picked.astype(jnp.float32), axis=1)
    return mixed.astype(jnp.bfloat16)


def solution(mesh):
    placed = (
        P(("grp", "exp", "ten"), None),
        P(),
        P(("grp", "exp", "ten"), None),
        P(("grp", "exp", "ten"), None),
        P("exp", None, "ten"),
        P("exp", None, "ten"),
        P("exp", "ten", None),
    )
    return jax.shard_map(
        per_device,
        mesh=mesh,
        in_specs=placed,
        out_specs=P(("grp", "exp", "ten"), None),
        check_vma=False,
    )
```

profile of v0, /device:TPU:26, one launch (start us, length us, event | category | flops | bytes accessed | tf_op | source)
XLA Modules:
  0.0 412.6 jit_solution(6275944661917493101)
XLA Ops:
  6.5 0.0 all-gather.3.cloned.1.call-start
  6.5 0.8 copy.19
  7.3 0.1 eq.40
  7.4 0.1 reshape.105
  7.5 0.6 reduce-window.6
  8.1 0.2 slice_reduce_fusion
  8.3 0.1 fusion.24
  8.4 0.1 reduce_sum.54
  8.5 0.2 fusion.18
  8.7 1.1 fusion.15
  9.8 2.0 convolution_convert_fusion
  11.8 42.1 %all_to_all.10 = bf16[8,2,24,4096]{3,2,1,0:T(8,128)(2,1)} all-to-all(bf16[8,2,24,4096]{3,2,1,0:T(8,128)(2,1)S(1)} %bitcast.71), channel_id=1, replica_groups=mesh['grp'=4,'exp'=8,'ten'=4] {'exp'}, dimensions={0} | all-to-all | bytes 6291456 | tf_op jit(solution)/shard_map/all_to_all | solution.py:39
  53.9 0.0 slice-start
  53.9 0.0 all-gather.3.cloned.1.call-update
  54.0 118.5 %all-gather.3.cloned.1.call-done = bf16[8,8,24,4096]{3,2,1,0:T(8,128)(2,1)} async-done(((bf16[8,2,24,4096]{3,2,1,0:T(8,128)(2,1)}), bf16[8,8,24,4096]{3,2,1,0:T(8,128)(2,1)}) %all-gather.3.cloned.1.call-update) | async-done | bytes 12582928 | tf_op jit(solution)/shard_map/all_gather | solution.py:42
  172.4 0.0 copy-start.1
  172.4 0.0 slice-start.1
  172.5 12.7 %fusion = f32[2,8,4,24,384]{4,3,2,1,0:T(8,128)} fusion(bf16[8,4,2,24,4096]{4,3,2,1,0:T(8,128)(2,1)} %bitcast.74, bf16[2,4096,384]{2,1,0:T(8,128)(2,1)} %param.12), kind=kOutput, calls=%fused_computation.3 | convolution fusion | flops 4831838208 | bytes 21233664 | tf_op jit(solution)/shard_map/abecd,edf->abecf/dot_general | solution.py:9
  185.1 0.0 slice-done
  185.1 0.0 copy-done.1
  185.1 0.0 slice-done.1
  185.1 8.5 %fusion.7 = bf16[8,4,2,24,384]{4,3,1,0,2:T(8,128)(2,1)S(1)} fusion(f32[2,8,4,24,384]{4,3,2,1,0:T(8,128)} %fusion, bf16[2,4096,384]{2,1,0:T(8,128)(2,1)S(1)} %bitcast.77, bf16[8,4,2,24,4096]{4,3,2,1,0:T(8,128)(2,1)S(1)} %bitcast.75), kind=kOutput, calls=%fused_computation.13 | convolution fusion | flops 4835377152 | bytes 22413312 | tf_op jit(solution)/shard_map/abecd,edf->abecf/dot_general | solution.py:8
  193.6 9.7 %convert_bitcast_fusion = bf16[8,4,2,24,4096]{4,3,1,0,2:T(8,128)(2,1)S(1)} fusion(bf16[8,4,2,24,384]{4,3,1,0,2:T(8,128)(2,1)S(1)} %fusion.7, bf16[2,384,4096]{2,1,0:T(8,128)(2,1)} %param.13), kind=kOutput, calls=%fused_computation.2 | convolution fusion | flops 4838129664 | bytes 20054016 | tf_op jit(solution)/shard_map/abecf,efd->abecd/dot_general | solution.py:11
  203.3 5.2 %copy.25 = bf16[8,4,2,24,4096]{4,3,2,1,0:T(8,128)(2,1)} copy(bf16[8,4,2,24,4096]{4,3,1,0,2:T(8,128)(2,1)S(1)} %convert_bitcast_fusion) | data formatting | bytes 25165824 | tf_op jit(solution)/shard_map/convert_element_type | solution.py:44
  208.5 0.0 copy-start
  208.5 8.2 %all-to-all-start.1 = ((bf16[32,48,4096]{2,1,0:T(8,128)(2,1)}), bf16[32,48,4096]{2,1,0:T(8,128)(2,1)}, u32[]{:S(2)}, u32[]{:S(2)}) async-start(bf16[32,48,4096]{2,1,0:T(8,128)(2,1)} %bitcast.70), calls=%async_computation.1 | async-start | bytes 25165824 | tf_op jit(solution)/shard_map/all_to_all | solution.py:47
  216.7 0.1 mul.71
  216.8 0.0 copy-done
  216.9 0.1 copy.18
  217.0 174.0 %all-to-all-done.1 = bf16[32,48,4096]{2,1,0:T(8,128)(2,1)} async-done(((bf16[32,48,4096]{2,1,0:T(8,128)(2,1)}), bf16[32,48,4096]{2,1,0:T(8,128)(2,1)}, u32[]{:S(2)}, u32[]{:S(2)}) %all-to-all-start.1) | async-done | bytes 12582944 | tf_op jit(solution)/shard_map/all_to_all | solution.py:47
  391.0 7.4 %bitcast_reduce_fusion = bf16[8,48,4096]{2,1,0:T(8,128)(2,1)S(1)} fusion(bf16[32,48,4096]{2,1,0:T(8,128)(2,1)} %all-to-all-done.1), kind=kLoop, calls=%fused_computation.1 | loop fusion | flops 4718592 | bytes 15728640 | tf_op jit(solution)/shard_map/reduce_sum | solution.py:49
  398.4 3.2 gather_fusion
  401.6 4.2 %multiply_reduce_fusion = bf16[32,4096]{1,0:T(8,128)(2,1)} fusion(bf16[256,4096]{1,0:T(8,128)(2,1)} %gather_fusion, f32[32,8]{1,0:T(8,128)S(1)} %copy.18, pred[32,8]{1,0:T(8,128)(4,1)S(1)} %get-tuple-element.5), kind=kLoop, calls=%fused_computation.11 | loop fusion | flops 4063232 | bytes 2360576 | tf_op jit(solution)/shard_map/reduce_sum | solution.py:52
  (11 shorter events, 0.1 us)
Async XLA Ops:
  6.5 165.9 %all-gather.3.cloned.1.call-start = ((), (), s32[]{:S(2)}) async-start(), calls=%async_computation.2 | async-start | bytes 15728640 | tf_op jit(solution)/shard_map/all_gather | solution.py:42
  53.9 131.2 %slice-start = ((s8[6291456]{0:T(1024)(128)(4,1)}), s8[2097152]{0:T(1024)(128)(4,1)S(1)}, s32[]{:S(2)}) async-start(s8[6291456]{0:T(1024)(128)(4,1)} %bitcast.76), calls=%async_computation.3 | async-start | bytes 4194304
  172.4 12.7 %copy-start.1 = (bf16[8,8,24,4096]{3,2,1,0:T(8,128)(2,1)S(1)}, bf16[8,8,24,4096]{3,2,1,0:T(8,128)(2,1)}, u32[]{:S(2)}) copy-start(bf16[8,8,24,4096]{3,2,1,0:T(8,128)(2,1)} %all-gather.3.cloned.1.call-done) | copy-start | bytes 37748740
  172.4 12.7 %slice-start.1 = ((s8[6291456]{0:T(1024)(128)(4,1)}), s8[4194304]{0:T(1024)(128)(4,1)S(1)}, s32[]{:S(2)}) async-start(s8[6291456]{0:T(1024)(128)(4,1)} %bitcast.76), calls=%async_computation.4 | async-start | bytes 8388608
  208.5 8.4 %copy-start = (f32[32,8]{0,1:T(8,128)S(1)}, f32[32,8]{0,1:T(8,128)}, u32[]{:S(2)}) copy-start(f32[32,8]{0,1:T(8,128)} %param.10) | copy-start | bytes 3076
  208.5 182.5 %all-to-all-start.1 = ((bf16[32,48,4096]{2,1,0:T(8,128)(2,1)}), bf16[32,48,4096]{2,1,0:T(8,128)(2,1)}, u32[]{:S(2)}, u32[]{:S(2)}) async-start(bf16[32,48,4096]{2,1,0:T(8,128)(2,1)} %bitcast.70), calls=%async_computation.1 | async-start | bytes 25165824 | tf_op jit(solution)/shard_map/all_to_all | solution.py:47
Sparse Core Ops, SparseCore 0:
  54.1 118.3 all-gather.2
where the time goes:
time: 413 us
  waiting for transfers between devices  292 us (71%)
  blocking collectives  42.1 us (10%)
  matrix products  32.8 us (8%)
  other arithmetic  13.7 us (3%)
  between operations  13.5 us (3%)
  local copies, waits for them, and re-layouts  9.78 us (2%)
  starting transfers between devices  8.24 us (2%)
    all_to_all x1, waiting for transfers between devices, per_device(): lax.all_to_all(sendback, ('exp', 'ten'), split_axis=0, concat_axis=0, til...  174 us
    all_gather x1, waiting for transfers between devices, per_device(): lax.all_gather(arrived, 'ten', axis=1, tiled=True)  118 us
    all_to_all x1, blocking collectives, per_device(): lax.all_to_all(outgoing, 'exp', split_axis=0, concat_axis=0, tiled=True)  42.1 us
    dot_general x1, matrix products, expert_pass(): jnp.einsum('abecd,edf->abecf', piece, w_up, preferred_element_type=jnp.fl...  12.7 us
    dot_general x1, matrix products, expert_pass(): jnp.einsum('abecf,efd->abecd', hidden, w_down, preferred_element_type=jnp...  9.7 us
    dot_general x1, matrix products, expert_pass(): jnp.einsum('abecd,edf->abecf', piece, w_gate, preferred_element_type=jnp....  8.45 us
  transfers between devices with their start and end apart: 2, of which 2 were waited for; matrix products, arithmetic and copies ran while one was open for 0% of the time, Pallas kernels for 0%

commit v1 on v0

v1 whole, which is shorter than its diff:
```python
import jax
import jax.numpy as jnp
from jax import lax
from jax.sharding import PartitionSpec as P


def per_device(tokens, norm_gain, expert_ids, gate_prob, w_gate, w_up, w_down):
    tok_rows, width = tokens.shape
    local_count, _, hid = w_gate.shape
    expert_count = local_count * lax.axis_size("exp")
    floats = tokens.astype(jnp.float32)
    meansq = jnp.mean(floats * floats, axis=1, keepdims=True)
    normed = (floats * lax.rsqrt(meansq + 1e-06) * norm_gain).astype(jnp.bfloat16)
    mixing = gate_prob / jnp.sum(gate_prob, axis=1, keepdims=True)
    chosen = expert_ids[:, :, None] == jnp.arange(expert_count, dtype=jnp.int32)[None, None, :]
    weight = jnp.sum(jnp.where(chosen, mixing[:, :, None], 0.0), axis=1)
    everyone = lax.all_gather(normed, ("exp", "ten"), axis=0, tiled=True)
    weights = lax.all_gather(weight, ("exp", "ten"), axis=0, tiled=True)
    mine = lax.dynamic_slice_in_dim(weights, lax.axis_index("exp") * local_count, local_count, axis=1)
    gate_part = jnp.einsum("td,edf->tef", everyone, w_gate, preferred_element_type=jnp.float32)
    up_part = jnp.einsum("td,edf->tef", everyone, w_up, preferred_element_type=jnp.float32)
    hidden = jax.nn.silu(gate_part) * up_part * mine[:, :, None]
    hidden = hidden.astype(jnp.bfloat16).reshape(-1, local_count * hid)
    partial = jnp.dot(hidden, w_down.reshape(local_count * hid, width), preferred_element_type=jnp.float32)
    return lax.psum_scatter(partial.astype(jnp.bfloat16), ("exp", "ten"), scatter_dimension=0, tiled=True)


def solution(mesh):
    placed = (
        P(("grp", "exp", "ten"), None),
        P(),
        P(("grp", "exp", "ten"), None),
        P(("grp", "exp", "ten"), None),
        P("exp", None, "ten"),
        P("exp", None, "ten"),
        P("exp", "ten", None),
    )
    return jax.shard_map(
        per_device,
        mesh=mesh,
        in_specs=placed,
        out_specs=P(("grp", "exp", "ten"), None),
        check_vma=False,
    )
```

time: 413 us -> 201 us (0.49)
  the two profiles are of different devices: /device:TPU:26 before, /device:TPU:0 now
where the time goes in v1:
time: 201 us
  waiting for transfers between devices  99.7 us (50%)
  blocking collectives  46 us (23%)
  matrix products  36.5 us (18%)
  between operations  13.4 us (7%)
  other arithmetic  5.01 us (2%)
    reduce_scatter x1, waiting for transfers between devices, per_device(): lax.psum_scatter(partial.astype(jnp.bfloat16), ('exp', 'ten'), scatter_di...  92.4 us
    all_gather x1, blocking collectives, per_device(): weights = lax.all_gather(weight, ('exp', 'ten'), axis=0, tiled=True)  46 us
    dot_general x1, matrix products, per_device(): jnp.dot(hidden, w_down.reshape(local_count * hid, width), preferred_eleme...  25.6 us
    dot_general x1, matrix products, per_device(): jnp.einsum('td,edf->tef', everyone, w_up, preferred_element_type=jnp.floa...  10.9 us
    all_gather x1, waiting for transfers between devices, per_device(): everyone = lax.all_gather(normed, ('exp', 'ten'), axis=0, tiled=True)  7.25 us
  transfers between devices with their start and end apart: 2, of which 2 were waited for; matrix products, arithmetic and copies ran while one was open for 1% of the time, Pallas kernels for 0%

profile of v1, /device:TPU:0, one launch (start us, length us, event | category | flops | bytes accessed | tf_op | source)
XLA Modules:
  0.0 201.0 jit_solution(15877539173031237271)
XLA Ops:
  6.5 0.0 all-gather.3.cloned.1.call-start
  6.5 1.1 fusion.10
  7.7 1.8 fusion.12
  9.4 0.0 all-gather.3.cloned.1.call-update
  9.5 0.0 reduce-scatter.2.cloned.1.call-start
  9.5 0.7 reduce_sum.28
  10.2 0.7 broadcast_divide_fusion
  10.9 0.7 select_reduce_fusion
  11.6 46.0 %all-gather = f32[32,32,16]{1,2,0:T(8,128)S(1)} all-gather(f32[1,32,16]{1,2,0:T(8,128)S(1)} %bitcast.17), channel_id=1, replica_groups=mesh['grp'=4,'exp'=8,'ten'=4] {'exp','ten'}, dimensions={0}, use_global_device_ids=true | all-gather | bytes 67584 | tf_op jit(solution)/shard_map/all_gather | solution.py:18
  57.7 0.1 copy.15
  57.7 0.1 reshape.16
  57.9 7.2 %all-gather.3.cloned.1.call-done = bf16[1024,4096]{1,0:T(8,128)(2,1)} async-done(((bf16[32,4096]{1,0:T(8,128)(2,1)}), bf16[1024,4096]{1,0:T(8,128)(2,1)}) %all-gather.3.cloned.1.call-update) | async-done | bytes 8388624 | tf_op jit(solution)/shard_map/all_gather | solution.py:17
  65.2 10.9 %fusion = f32[1024,2,384]{2,0,1:T(8,128)S(1)} fusion(bf16[2,4096,384]{2,1,0:T(8,128)(2,1)} %param.12, bf16[1024,4096]{1,0:T(8,128)(2,1)} %all-gather.3.cloned.1.call-done), kind=kOutput, calls=%fused_computation.1 | convolution fusion | flops 6442450944 | bytes 17825792 | tf_op jit(solution)/shard_map/td,edf->tef/dot_general | solution.py:21
  76.1 25.6 %bitcast_convert_fusion = bf16[1024,4096]{1,0:T(8,128)(2,1)} fusion(bf16[2,384,4096]{2,1,0:T(8,128)(2,1)} %param.13, f32[1024,2,384]{2,0,1:T(8,128)S(1)} %fusion, bf16[2,4096,384]{2,1,0:T(8,128)(2,1)} %param.11, bf16[1024,4096]{1,0:T(8,128)(2,1)} %all-gather.3.cloned.1.call-done, f32[1024,2]{0,1:T(2,128)S(1)} %constant_dynamic-slice_fusion), kind=kOutput, calls=%fused_computation | convolution fusion | flops 12894601216 | bytes 32514048 | tf_op jit(solution)/shard_map/dot_general | solution.py:24
  101.7 0.0 reduce-scatter.2.cloned.1.call-update
  101.7 92.4 %reduce-scatter.2.cloned.1.call-done = bf16[32,4096]{1,0:T(8,128)(2,1)} async-done(((bf16[1024,4096]{1,0:T(8,128)(2,1)}), bf16[32,4096]{1,0:T(8,128)(2,1)}) %reduce-scatter.2.cloned.1.call-update) | async-done | bytes 262160 | tf_op jit(solution)/shard_map/reduce_scatter | solution.py:25
  (2 shorter events, 0.0 us)
Async XLA Ops:
  6.5 58.6 %all-gather.3.cloned.1.call-start = ((), (), s32[]{:S(2)}) async-start(), calls=%async_computation.1 | async-start | bytes 8650752 | tf_op jit(solution)/shard_map/all_gather | solution.py:17
  9.5 184.7 %reduce-scatter.2.cloned.1.call-start = ((), (), s32[]{:S(2)}) async-start(), calls=%async_computation.2 | async-start | bytes 8650752 | tf_op jit(solution)/shard_map/reduce_scatter | solution.py:25
Sparse Core Ops, SparseCore 0:
  9.6 55.5 all-gather.2
  101.8 92.2 reduce-scatter.1

commit v2 on v1

v2 whole, which is shorter than its diff:
```python
import functools

import jax
import jax.numpy as jnp
from jax import lax
from jax.experimental import pallas as pl
from jax.experimental.pallas import tpu as pltpu
from jax.sharding import PartitionSpec as P

MESH = pl.DeviceIdType.MESH
BF16, F32 = jnp.bfloat16, jnp.float32
SIDE = 4
ROWS = 16
EXTRA = 128
PIECES = 4
DIRS = (1, -1)
ORDER = (0, 1, 3, 2)
RATE, SIB_RATE = 46.5e3, 200e3
LAT, SIB_LAT = 1.7, 1.1
T_UP, T_DOWN, T_ADD = 1.75, 0.55, 0.12


def fw(d):
    return 0 if d == 1 else 1


def toward(h):
    return 1 if h == 0 else -1


def axis_of(s, second):
    return (s + second) % 2


def plan(width):
    block = ROWS * width * 2
    msgs = {}
    tasks = {}

    def msg(key, link, size):
        msgs[key] = (link, size)

    def task(key, needs, after, dur, sends, prio):
        tasks[key] = (needs, after, dur, sends, prio)

    rank = {df: i for i, df in enumerate(ORDER)}
    for s in (0, 1):
        for d in DIRS:
            for h in (0, 1):
                msg(("m1", s, d, h), (axis_of(s, 0), d), block / 2)
                msg(("r4", s, d, h), (axis_of(s, 0), d), block / 2)
            msg(("m2", s, d), (axis_of(s, 0), d), block / 2)
            msg(("r3", s, d), (axis_of(s, 0), d), block / 2)
            for df in range(SIDE):
                for h in (0, 1):
                    msg(("m3", df, s, d, h), (axis_of(s, 1), d), block / 2)
                    msg(("r2", df, s, d, h), (axis_of(s, 1), d), block / 2)
                msg(("m4", df, s, d), (axis_of(s, 1), d), block / 2)
                msg(("r1", df, s, d), (axis_of(s, 1), d), block / 2)
        for df in range(SIDE):
            for dg in range(SIDE):
                msg(("m5", df, s, dg), "sib", block)
    for df in range(SIDE):
        for n in range(PIECES):
            msg(("r0", df, n), "sib", 8 * block / PIECES)

    first = []
    for h in (0, 1):
        for s in (0, 1):
            first += [("m3", 0, s, d, h if d == 1 else 1 - h) for d in DIRS]
    for h in (0, 1):
        for s in (0, 1):
            first += [("m1", s, d, h if d == 1 else 1 - h) for d in DIRS]
    first += [("m5", 0, s, 0) for s in (0, 1)]
    task(("own",), [], [], 0.0, first, (-1,))
    for s in (0, 1):
        for d in DIRS:
            for h in (0, 1):
                df = -d % SIDE
                ahead = [("m2", s, d)] if h == fw(d) else []
                onward = [("m3", df, s, toward(h), h), ("m3", df, s, -toward(h), h)]
                task(("a1", s, d, h), [("m1", s, d, h)], [], 0.0, ahead + onward, (0, rank[df]))
            h = fw(d)
            onward = [("m3", 2, s, toward(h), h), ("m3", 2, s, -toward(h), h)]
            task(("a2", s, d), [("m2", s, d)], [], 0.0, onward, (0, rank[2]))
            for df in range(SIDE):
                task(("a3", df, s, d), [("m3", df, s, d, fw(d))], [], 0.0, [("m4", df, s, d)], (0, rank[df]))
        for df in range(SIDE):
            for dg in range(SIDE):
                if dg == 2:
                    needs = [("m4", df, s, d) for d in DIRS]
                elif dg:
                    needs = [("m3", df, s, 1 if dg == 3 else -1, h) for h in (0, 1)]
                elif df == 2:
                    needs = [("m2", s, d) for d in DIRS]
                elif df:
                    needs = [("m1", s, 1 if df == 3 else -1, h) for h in (0, 1)]
                else:
                    continue
                task(("a5", df, s, dg), needs, [], 0.0, [("m5", df, s, dg)], (1, rank[df]))
    for df in range(SIDE):
        blocks = [("m5", df, s, dg) for s in (0, 1) for dg in range(SIDE)]
        sent = [("a5",) + b[1:] for b in blocks if b[1] or b[3]]
        for l in (0, 1):
            task(("U", df, l), blocks, sent + ([("U", df, 0)] if l else []), T_UP, [], (9, rank[df], 0, l))
        for n in range(PIECES):
            before = [("D", df, n - 1)] if n else [("U", df, 1)]
            task(("D", df, n), [], before, T_DOWN, [("r0", df, n)], (9, rank[df], 1, n))
        for h in (0, 1):
            t = toward(h)
            parts = range(h * PIECES // 2, (h + 1) * PIECES // 2)
            sends = [("r1", df, s, t) for s in (0, 1)] + [("r2", df, s, -t, h) for s in (0, 1)]
            task(("p2", df, h), [("r0", df, n) for n in parts], [], 4 * T_ADD, sends, (3, rank[df]))
            for s in (0, 1):
                after = [("p2", df, h)]
                task(("p13", df, s, h), [("r1", df, s, t)], after, T_ADD, [("r2", df, s, t, h)], (2, rank[df]))
                needs = [("r2", df, s, d, h) for d in DIRS]
                if df == 2:
                    sends = [("r3", s, t)]
                elif df:
                    d = 1 if df == 1 else -1
                    if h == fw(d):
                        needs = needs + [("r3", s, d)]
                    sends = [("r4", s, d, h)]
                else:
                    needs = needs + [("r4", s, d, h) for d in DIRS]
                    sends = []
                task(("p0", df, s, h), needs, after, T_ADD, sends, (2, rank[df]))

    free = {}
    arrive = {}
    done = {}
    order = []
    now = 0.0
    pending = dict(tasks)
    while pending:
        best = None
        for key, (needs, after, dur, sends, prio) in pending.items():
            if any(n not in arrive for n in needs) or any(a not in done for a in after):
                continue
            at = max([now] + [arrive[n] for n in needs])
            rankkey = (at, prio, str(key))
            if best is None or rankkey < best[0]:
                best = (rankkey, key)
        (at, _, _), key = best
        needs, after, dur, sends, prio = pending.pop(key)
        now = at + dur + 0.01
        done[key] = now
        order.append(key)
        for m in sends:
            link, size = msgs[m]
            rate, lat = (SIB_RATE, SIB_LAT) if link == "sib" else (RATE, LAT)
            end = max(free.get(link, 0.0), now) + size / rate
            free[link] = end
            arrive[m] = end + lat
    return order, tasks, list(msgs), now, done, free


def kernel(order, tasks, names, tokens, gain, ids, prob, wg, wu, wd, out,
           xbuf, w1, w2, hid, ybuf, sib, halves, fulls, halves2, fulls2, wsem, ssem, rsem):
    exp, ten = lax.axis_index("exp"), lax.axis_index("ten")
    cx, core = exp // 2, exp % 2
    width = tokens.shape[1]
    half = width // 2
    hidden = wg.shape[2]
    local = wg.shape[0]
    xcut = (width + EXTRA) // 256 * 128 + 128

    def device(axis, d):
        if axis == 0:
            return {"exp": (cx + SIDE + d) % SIDE * 2 + core, "ten": ten}
        return {"exp": exp, "ten": (ten + SIDE + d) % SIDE}

    other = {"exp": cx * 2 + 1 - core, "ten": ten}
    partners = [device(a, d) for a in (0, 1) for d in DIRS] + [other]
    barrier = pltpu.get_barrier_semaphore()
    for p in partners:
        pl.semaphore_signal(barrier, inc=1, device_id=p, device_id_type=MESH)

    loads = []
    for l in range(local):
        loads.append(pltpu.make_async_copy(wg.at[l], w1.at[l, :, pl.ds(0, hidden)], wsem.at[3 * l]))
        loads.append(pltpu.make_async_copy(wu.at[l], w1.at[l, :, pl.ds(hidden, hidden)], wsem.at[3 * l + 1]))
    for l in range(local):
        loads.append(pltpu.make_async_copy(wd.at[l], w2.at[pl.ds(l * hidden, hidden)], wsem.at[3 * l + 2]))
    for c in loads:
        c.start()

    def rows(k, s, dg):
        return pl.ds(((k * 2 + s) * SIDE + dg % SIDE) * ROWS, ROWS)

    def xcols(h):
        return pl.ds(0, xcut) if h == 0 else pl.ds(xcut, width + EXTRA - xcut)

    def ycols(h):
        return pl.ds(h * half, half)

    def xat(df, k, s, dg, h=None):
        if h is None:
            return xbuf.at[df % SIDE, rows(k, s, dg)]
        return xbuf.at[df % SIDE, rows(k, s, dg), xcols(h)]

    def yat(df, k, s, dg, h):
        return ybuf.at[df % SIDE, rows(k, s, dg), ycols(h)]

    def ends(key):
        kind = key[0]
        if kind == "m1":
            _, s, d, h = key
            return xat(0, 0, s, 0, h), xat(-d, 0, s, 0, h), device(axis_of(s, 0), d)
        if kind == "m2":
            _, s, d = key
            return xat(-d, 0, s, 0, fw(d)), xat(2, 0, s, 0, fw(d)), device(axis_of(s, 0), d)
        if kind == "m3":
            _, df, s, d, h = key
            return xat(df, 0, s, 0, h), xat(df, 0, s, -d, h), device(axis_of(s, 1), d)
        if kind == "m4":
            _, df, s, d = key
            return xat(df, 0, s, -d, fw(d)), xat(df, 0, s, 2, fw(d)), device(axis_of(s, 1), d)
        if kind == "m5":
            _, df, s, dg = key
            return xat(df, 0, s, dg), xat(df, 1, s, dg), other
        if kind == "r0":
            _, df, n = key
            part = pl.ds(n * (width // PIECES), width // PIECES)
            return ybuf.at[df, pl.ds(8 * ROWS, 8 * ROWS), part], sib.at[df, :, part], other
        if kind == "r1":
            _, df, s, d = key
            return yat(df, 0, s, 2, fw(d)), halves.at[df, s, fw(d)], device(axis_of(s, 1), d)
        if kind == "r2":
            _, df, s, d, h = key
            return yat(df, 0, s, d, h), fulls.at[df, s, fw(d), :, ycols(h)], device(axis_of(s, 1), d)
        if kind == "r3":
            _, s, d = key
            return yat(2, 0, s, 0, fw(d)), halves2.at[s, fw(d)], device(axis_of(s, 0), d)
        _, s, d, h = key
        return yat(d, 0, s, 0, h), fulls2.at[s, fw(d), :, ycols(h)], device(axis_of(s, 0), d)

    index = {key: i for i, key in enumerate(names)}

    def copy(key):
        src, dst, dev = ends(key)
        i = index[key]
        return pltpu.make_async_remote_copy(
            src_ref=src, dst_ref=dst, send_sem=ssem.at[i], recv_sem=rsem.at[i],
            device_id=dev, device_id_type=MESH)

    floats = tokens[...].astype(F32)
    meansq = jnp.mean(floats * floats, axis=1, keepdims=True)
    normed = (floats * lax.rsqrt(meansq + 1e-06) * gain[...]).astype(BF16)
    mixing = prob[...] / jnp.sum(prob[...], axis=1, keepdims=True)
    lane = lax.broadcasted_iota(jnp.int32, (2 * ROWS, EXTRA), 1)
    experts = local * SIDE * 2
    mix = jnp.zeros((2 * ROWS, EXTRA), F32)
    chosen = ids[...]
    for k in range(chosen.shape[1]):
        mine = jnp.broadcast_to(chosen[:, k:k + 1], lane.shape)
        mine = (mine == lane) | (mine + experts == lane)
        mix = mix + jnp.where(mine, jnp.broadcast_to(mixing[:, k:k + 1], lane.shape), 0.0)
    coarse = mix.astype(BF16)
    fine = (mix - coarse.astype(F32)).astype(BF16)
    packed = jnp.where(lane < experts, coarse.astype(F32), fine.astype(F32)).astype(BF16)
    for s in (0, 1):
        xbuf[0, rows(0, s, 0), pl.ds(0, width)] = normed[s * ROWS:(s + 1) * ROWS]
        xbuf[0, rows(0, s, 0), pl.ds(width, EXTRA)] = packed[s * ROWS:(s + 1) * ROWS]
    pl.semaphore_wait(barrier, len(partners))

    line = lax.broadcasted_iota(jnp.int32, (EXTRA, EXTRA), 0)

    def up(df, l):
        both = jnp.dot(xbuf[df, :, pl.ds(0, width)], w1[l], preferred_element_type=F32)
        e = exp * local + l
        pick = jnp.where((line == e) | (line == e + experts), 1.0, 0.0).astype(BF16)
        weight = jnp.dot(xbuf[df, :, pl.ds(width, EXTRA)], pick, preferred_element_type=F32)
        for c in range(0, hidden, EXTRA):
            g, u = both[:, c:c + EXTRA], both[:, hidden + c:hidden + c + EXTRA]
            hid[:, pl.ds(l * hidden + c, EXTRA)] = (g / (1.0 + jnp.exp(-g)) * u * weight).astype(BF16)

    def down(df, n):
        part = pl.ds(n * (width // PIECES), width // PIECES)
        ybuf[df, :, part] = jnp.dot(hid[...], w2[:, part], preferred_element_type=F32).astype(BF16)

    def total(df, s, dg, h):
        own = ybuf[df, rows(0, s, dg), ycols(h)].astype(F32)
        return own + sib[df, rows(0, s, dg), ycols(h)].astype(F32)

    got = set()
    loaded = set()

    def load_wait(which):
        for i in which:
            if i not in loaded:
                loaded.add(i)
                loads[i].wait()

    for key in order:
        needs, after, dur, sends, prio = tasks[key]
        for m in needs:
            if m not in got:
                got.add(m)
                copy(m).wait_recv()
        kind = key[0]
        if kind == "U":
            load_wait((2 * key[2], 2 * key[2] + 1))
            up(key[1], key[2])
        elif kind == "D":
            load_wait((4, 5))
            down(key[1], key[2])
        elif kind == "p2":
            _, df, h = key
            for s in (0, 1):
                ybuf[df, rows(0, s, 2), ycols(h)] = total(df, s, 2, h).astype(BF16)
            for s in (0, 1):
                ybuf[df, rows(0, s, -toward(h)), ycols(h)] = total(df, s, -toward(h), h).astype(BF16)
        elif kind == "p13":
            _, df, s, h = key
            t = toward(h)
            ybuf[df, rows(0, s, t), ycols(h)] = (total(df, s, t, h) + halves[df, s, h].astype(F32)).astype(BF16)
        elif kind == "p0":
            _, df, s, h = key
            whole = total(df, s, 0, h)
            for i in (0, 1):
                whole = whole + fulls[df, s, i, :, ycols(h)].astype(F32)
            if df == 0:
                for i in (0, 1):
                    whole = whole + fulls2[s, i, :, ycols(h)].astype(F32)
                out[pl.ds(s * ROWS, ROWS), ycols(h)] = whole.astype(BF16)
            else:
                if df != 2 and h == fw(1 if df == 1 else -1):
                    whole = whole + halves2[s, h].astype(F32)
                ybuf[df, rows(0, s, 0), ycols(h)] = whole.astype(BF16)
        for m in sends:
            copy(m).start()
    for m in names:
        copy(m).wait_send()


def per_device(tokens, norm_gain, expert_ids, gate_prob, w_gate, w_up, w_down):
    count, width = tokens.shape
    local, _, hidden = w_gate.shape
    order, tasks, names, _, _, _ = plan(width)
    vmem = pl.BlockSpec(memory_space=pltpu.VMEM)
    hbm = pl.BlockSpec(memory_space=pl.ANY)
    chunk = 2 * 2 * SIDE * ROWS
    return pl.pallas_call(
        functools.partial(kernel, order, tasks, names),
        out_shape=jax.ShapeDtypeStruct((count, width), BF16),
        in_specs=[vmem] * 4 + [hbm] * 3,
        out_specs=vmem,
        scratch_shapes=[
            pltpu.VMEM((SIDE, chunk, width + EXTRA), BF16),
            pltpu.VMEM((local, width, 2 * hidden), BF16),
            pltpu.VMEM((local * hidden, width), BF16),
            pltpu.VMEM((chunk, local * hidden), BF16),
            pltpu.VMEM((SIDE, chunk, width), BF16),
            pltpu.VMEM((SIDE, chunk // 2, width), BF16),
            pltpu.VMEM((SIDE, 2, 2, ROWS, width // 2), BF16),
            pltpu.VMEM((SIDE, 2, 2, ROWS, width), BF16),
            pltpu.VMEM((2, 2, ROWS, width // 2), BF16),
            pltpu.VMEM((2, 2, ROWS, width), BF16),
            pltpu.SemaphoreType.DMA((3 * local,)),
            pltpu.SemaphoreType.DMA((len(names),)),
            pltpu.SemaphoreType.DMA((len(names),)),
        ],
        compiler_params=pltpu.CompilerParams(
            collective_id=0, has_side_effects=True, vmem_limit_bytes=60 * 1024 * 1024),
        name="experts",
    )(tokens, norm_gain.reshape(1, width), expert_ids, gate_prob, w_gate, w_up, w_down)


def solution(mesh):
    placed = (
        P(("grp", "exp", "ten"), None),
        P(),
        P(("grp", "exp", "ten"), None),
        P(("grp", "exp", "ten"), None),
        P("exp", None, "ten"),
        P("exp", None, "ten"),
        P("exp", "ten", None),
    )
    return jax.shard_map(
        per_device,
        mesh=mesh,
        in_specs=placed,
        out_specs=P(("grp", "exp", "ten"), None),
        check_vma=False,
    )
```

time: 201 us -> 83.7 us (0.42)
  waiting for transfers between devices: 99.7 us -> 0 us
  Pallas kernels: 0 us -> 79.1 us
  blocking collectives: 46 us -> 0 us
  matrix products: 36.5 us -> 0 us
  between operations: 13.4 us -> 0.01 us
  other arithmetic: 5.01 us -> 0 us
  local copies, waits for them, and re-layouts: 0.24 us -> 4.39 us
    reduce_scatter x1 -> x0, waiting for transfers between devices: 92.4 us -> none  [per_device(): lax.psum_scatter(partial.astype(jnp.bfloat16), ('exp', 'ten'), scatter_di...]
    pallas_call x0 -> x1, Pallas kernels: none -> 79.1 us  [per_device(): pl.pallas_call(functools.partial(kernel, order, tasks, names), out_shape=...]
    all_gather x1 -> x0, blocking collectives: 46 us -> none  [per_device(): weights = lax.all_gather(weight, ('exp', 'ten'), axis=0, tiled=True)]
    dot_general x2 -> x0, matrix products: 36.5 us -> none  [the longest x1 25.6 us: per_device(): jnp.dot(hidden, w_down.reshape(local_count * hid, width), preferred_eleme...]
    all_gather x1 -> x0, waiting for transfers between devices: 7.25 us -> none  [per_device(): everyone = lax.all_gather(normed, ('exp', 'ten'), axis=0, tiled=True)]
    unnamed x1 -> x3, local copies, waits for them, and re-layouts: 0.14 us -> 4.39 us
    reduce_sum x3 -> x0, other arithmetic: 2.52 us -> none  [the longest x1 1.11 us: per_device(): meansq = jnp.mean(floats * floats, axis=1, keepdims=True)]
  transfers between devices with their start and end apart: 2 -> 0, of which waited for: 2 -> 0; matrix products, arithmetic and copies ran while one was open for 1% -> 0% of each run, Pallas kernels for 0% -> 0%
where the time goes in v2:
time: 83.7 us; the launch traced here: 83.5 us
  Pallas kernels  79.1 us (95%)
  local copies, waits for them, and re-layouts  4.39 us (5%)
    pallas_call x1, Pallas kernels, per_device(): pl.pallas_call(functools.partial(kernel, order, tasks, names), out_shape=...  79.1 us
    unnamed x3, local copies, waits for them, and re-layouts  4.39 us

profile of v2, /device:TPU:0, one launch (start us, length us, event | category | flops | bytes accessed | tf_op | source)
XLA Modules:
  0.0 83.5 jit_solution(3287603769251558743)
XLA Ops:
  0.0 1.4 %copy.8.ids = s32[32,8]{1,0:T(8,128)} copy(s32[32,8]{0,1:T(8,128)} %param.9) | data formatting | bytes 2048 | tf_op args[2]
  1.4 1.4 %copy.9.prob = f32[32,8]{1,0:T(8,128)} copy(f32[32,8]{0,1:T(8,128)} %param.10) | data formatting | bytes 2048 | tf_op args[3]
  2.7 79.1 %experts.1 = bf16[32,4096]{1,0:T(8,128)(2,1)} custom-call(bf16[32,4096]{1,0:T(8,128)(2,1)} %tokens.1, f32[1,4096]{1,0:T(1,128)} %bitcast.1, s32[32,8]{1,0:T(8,128)} %copy.8.ids, f32[32,8]{1,0:T(8,128)} %copy.9.prob, bf16[2,4096,384]{2,1,0:T(8,128)(2,1)} %wg.1, bf16[2,4096,384]{2,1,0:T(8,128)(2,1)} %wu.1, bf16[2,384,4096]{2,1,0:T(8,128)(2,1)} %wd.1), custom_call_target="tpu_custom_call" | custom-call | tf_op jit(solution)/shard_map/experts/pallas_call | solution.py:345
  81.8 1.7 %copy.11 = bf16[32,4096]{1,0:T(8,128)(2,1)} copy(bf16[32,4096]{1,0:T(8,128)(2,1)} %experts.1) | data formatting | bytes 524288

commit v3 on v1

v3 whole, which is shorter than its diff:
```python
import functools

import jax
import jax.numpy as jnp
from jax import lax
from jax.experimental import pallas as pl
from jax.experimental.pallas import tpu as pltpu
from jax.sharding import PartitionSpec as P

MESH = pl.DeviceIdType.MESH
BF16, F32 = jnp.bfloat16, jnp.float32
SIDE = 4
ROWS = 16
EXTRA = 128
PIECES = 4
DIRS = (1, -1)
ORDER = (
    ("m3", 0, 1, 1, 0), ("m1", 0, 1, 0), ("m1", 0, 1, 1), ("m1", 1, 1, 1), ("m3", 0, 1, -1, 1), ("m3", 0, 0, 1, 0),
    ("m1", 1, 1, 0), ("m5", 0, 0, 0), ("m3", 0, 1, 1, 1), ("m3", 0, 0, -1, 1), ("m5", 0, 1, 0), ("m3", 0, 1, -1, 0),
    ("m1", 1, -1, 1), ("m1", 0, -1, 1), ("m3", 0, 0, -1, 0), ("m3", 0, 0, 1, 1), ("m4", 0, 0, -1), ("m5", 0, 1, 1),
    ("m4", 0, 1, -1), ("m4", 0, 1, 1), ("m3", 3, 0, -1, 1), ("m4", 0, 0, 1), ("m3", 3, 0, -1, 0), ("m3", 3, 1, 1, 0),
    ("m3", 3, 1, -1, 1), ("m3", 3, 1, -1, 0), ("m2", 1, -1), ("m2", 0, -1), ("m3", 3, 0, 1, 0), ("m5", 0, 0, 1),
    ("m1", 0, -1, 0), ("m2", 1, 1), ("m5", 3, 0, 0), ("m3", 3, 0, 1, 1), ("m2", 0, 1), ("m5", 0, 0, 3),
    ("m5", 0, 1, 3), ("m5", 0, 1, 2), ("m4", 3, 0, -1), ("m1", 1, -1, 0), ("m3", 3, 1, 1, 1), ("m5", 0, 0, 2),
    ("m4", 3, 1, 1), ("m4", 3, 0, 1), ("m4", 3, 1, -1), ("m5", 3, 0, 1), ("U", 0, 0), ("m5", 2, 0, 0),
    ("m3", 2, 0, -1, 1), ("m3", 2, 1, -1, 1), ("m3", 1, 1, -1, 1), ("m5", 2, 1, 0), ("m5", 3, 1, 1),
    ("m3", 2, 1, -1, 0), ("m3", 2, 0, 1, 0), ("m3", 2, 0, 1, 1), ("m5", 3, 1, 0), ("m3", 2, 1, 1, 1),
    ("m3", 2, 0, -1, 0), ("m3", 1, 0, -1, 1), ("m3", 2, 1, 1, 0), ("m5", 3, 1, 3), ("U", 0, 1), ("m5", 3, 0, 2),
    ("m3", 1, 1, 1, 1), ("m5", 3, 0, 3), ("m5", 3, 1, 2), ("D", 0, 0), ("D", 0, 3), ("r0", 0, 0), ("m3", 1, 1, 1, 0),
    ("r0", 0, 3), ("D", 0, 1), ("r0", 0, 1), ("m4", 2, 0, 1), ("D", 0, 2), ("r0", 0, 2), ("m5", 1, 0, 0),
    ("m3", 1, 0, 1, 1), ("m3", 1, 0, 1, 0), ("m4", 2, 1, -1), ("m4", 2, 0, -1), ("m4", 2, 1, 1), ("U", 3, 1),
    ("m5", 2, 0, 1), ("m5", 2, 1, 3), ("U", 3, 0), ("m5", 2, 0, 3), ("q", 0, 1, 2, 0), ("r1", 0, 1, 1),
    ("m5", 1, 1, 0), ("m3", 1, 1, -1, 0), ("D", 3, 3), ("q", 0, 1, -1, 0), ("m5", 2, 0, 2), ("m4", 1, 0, -1),
    ("q", 0, 1, 2, 1), ("m5", 2, 1, 2), ("m5", 2, 1, 1), ("m3", 1, 0, -1, 0), ("q", 0, 0, -1, 0), ("q", 0, 0, 2, 1),
    ("D", 3, 2), ("q", 0, 1, 1, 1), ("r0", 3, 2), ("r1", 0, 1, -1), ("D", 3, 1), ("r0", 3, 1), ("m4", 1, 1, 1),
    ("m4", 1, 0, 1), ("q", 0, 0, 1, 1), ("D", 3, 0), ("r0", 3, 3), ("q", 0, 1, 1, 0), ("r2", 0, 1, 1, 1),
    ("r2", 0, 1, -1, 0), ("r2", 0, 1, 1, 0), ("m5", 1, 1, 1), ("q", 0, 0, 2, 0), ("r1", 0, 0, 1), ("m4", 1, 1, -1),
    ("U", 2, 0), ("r0", 3, 0), ("U", 2, 1), ("m5", 1, 0, 3), ("q", 3, 0, 2, 1), ("r1", 3, 0, -1), ("m5", 1, 0, 1),
    ("q", 0, 1, -1, 1), ("q", 3, 1, 1, 1), ("m5", 1, 1, 3), ("D", 2, 1), ("m5", 1, 0, 2), ("q", 3, 1, 2, 0),
    ("r2", 0, 0, 1, 1), ("q", 3, 0, -1, 0), ("r2", 3, 0, -1, 0), ("r2", 0, 1, -1, 1), ("r2", 0, 0, -1, 0),
    ("q", 3, 0, 1, 1), ("m5", 1, 1, 2), ("q", 3, 0, 2, 0), ("r1", 3, 0, 1), ("r1", 3, 1, 1), ("r0", 2, 1),
    ("q", 3, 1, -1, 0), ("D", 2, 2), ("r2", 3, 1, -1, 0), ("D", 2, 0), ("r2", 3, 1, 1, 1), ("r2", 3, 0, 1, 1),
    ("r0", 2, 0), ("D", 2, 3), ("r0", 2, 3), ("r1", 0, 0, -1), ("r0", 2, 2), ("U", 1, 1), ("q", 2, 1, 2, 0),
    ("r1", 2, 1, 1), ("q", 2, 1, -1, 0), ("r2", 2, 1, -1, 0), ("q", 2, 0, 2, 0), ("r1", 2, 0, 1), ("q", 3, 0, 1, 0),
    ("r2", 3, 0, 1, 0), ("q", 3, 0, -1, 1), ("r2", 3, 0, -1, 1), ("q", 3, 1, 2, 1), ("r1", 3, 1, -1), ("U", 1, 0),
    ("D", 1, 3), ("r0", 1, 3), ("q", 2, 0, 2, 1), ("r1", 2, 0, -1), ("q", 2, 1, 2, 1), ("r1", 2, 1, -1), ("D", 1, 2),
    ("r0", 1, 2), ("q", 2, 0, 1, 1), ("r2", 2, 0, 1, 1), ("q", 3, 1, 1, 0), ("r2", 3, 1, 1, 0), ("q", 2, 0, -1, 0),
    ("r2", 2, 0, -1, 0), ("D", 1, 1), ("q", 2, 1, 1, 0), ("r0", 1, 1), ("q", 3, 1, -1, 1), ("r2", 3, 1, -1, 1),
    ("q", 2, 0, 1, 0), ("r2", 2, 1, 1, 0), ("r2", 2, 0, 1, 0), ("D", 1, 0), ("r0", 1, 0), ("q", 1, 0, 2, 1),
    ("r1", 1, 0, -1), ("q", 2, 0, -1, 1), ("r2", 2, 0, -1, 1), ("q", 1, 1, 2, 1), ("r1", 1, 1, -1),
    ("q", 1, 0, 1, 1), ("r2", 1, 0, 1, 1), ("q", 2, 1, 1, 1), ("q", 2, 1, -1, 1), ("r2", 2, 1, 1, 1),
    ("r2", 2, 1, -1, 1), ("q", 1, 0, -1, 0), ("r2", 1, 0, -1, 0), ("q", 1, 1, 2, 0), ("r1", 1, 1, 1),
    ("q", 1, 0, 2, 0), ("r1", 1, 0, 1), ("q", 2, 0, 0, 0), ("q", 2, 1, 0, 0), ("q", 1, 0, -1, 1), ("r3", 1, 1),
    ("r2", 1, 0, -1, 1), ("q", 0, 0, -1, 1), ("q", 1, 1, -1, 1), ("r2", 1, 1, -1, 1), ("r3", 0, 1),
    ("q", 1, 1, -1, 0), ("q", 2, 0, 0, 1), ("r3", 0, -1), ("q", 1, 1, 1, 1), ("r2", 1, 1, 1, 1), ("q", 2, 1, 0, 1),
    ("r3", 1, -1), ("r2", 1, 1, -1, 0), ("r2", 0, 0, -1, 1), ("q", 1, 1, 1, 0), ("q", 1, 0, 1, 0),
    ("r2", 1, 0, 1, 0), ("q", 0, 0, 1, 0), ("r2", 0, 0, 1, 0), ("q", 3, 1, 0, 0), ("q", 3, 0, 0, 0),
    ("r2", 1, 1, 1, 0), ("r4", 0, -1, 0), ("r4", 1, -1, 0), ("q", 1, 0, 0, 1), ("r4", 0, 1, 1), ("q", 1, 1, 0, 1),
    ("r4", 1, 1, 1), ("q", 3, 1, 0, 1), ("q", 3, 0, 0, 1), ("r4", 1, -1, 1), ("q", 1, 0, 0, 0), ("r4", 0, -1, 1),
    ("r4", 0, 1, 0), ("q", 1, 1, 0, 0), ("r4", 1, 1, 0), ("q", 0, 0, 0, 1), ("q", 0, 0, 0, 0), ("q", 0, 1, 0, 1),
    ("q", 0, 1, 0, 0),
)
SENT = tuple(k for k in ORDER if k[0] not in ("U", "D", "q"))


def fw(d):
    return 0 if d == 1 else 1


def toward(h):
    return 1 if h == 0 else -1


def axis_of(s, second):
    return (s + second) % 2


def gathered(df, s, dg):
    if dg == 2:
        return [("m4", df, s, d) for d in DIRS]
    if dg:
        return [("m3", df, s, 1 if dg == 3 else -1, h) for h in (0, 1)]
    if df == 2:
        return [("m2", s, d) for d in DIRS]
    return [("m1", s, 1 if df == 3 else -1, h) for h in (0, 1)] if df else []


def needs(key):
    kind = key[0]
    if kind == "m2":
        return [("m1", key[1], key[2], fw(key[2]))]
    if kind == "m3":
        _, df, s, d, h = key
        return [m for m in gathered(df, s, 0) if (fw(m[2]) if m[0] == "m2" else m[3]) == h]
    if kind == "m4":
        return [("m3", key[1], key[2], key[3], fw(key[3]))]
    if kind == "m5":
        return gathered(*key[1:])
    if kind == "U":
        found = []
        for s in (0, 1):
            for dg in range(SIDE):
                found += gathered(key[1], s, dg) + [("m5", key[1], s, dg)]
        return found
    if kind == "q":
        _, df, s, dg, h = key
        t = toward(h)
        found = [("r0", df, n) for n in range(h * PIECES // 2, (h + 1) * PIECES // 2)]
        if dg == t:
            found.append(("r1", df, s, t))
        if dg == 0:
            found += [("r2", df, s, d, h) for d in DIRS]
            if df == 0:
                found += [("r4", s, d, h) for d in DIRS]
            elif df == t % SIDE:
                found.append(("r3", s, t))
        return found
    return []


def kernel(tokens_hbm, gain_hbm, ids_hbm, prob_hbm, wg, wu, wd, out, tokens, gain, ids, prob,
           xbuf, w1, w2, hid, ybuf, sib, halves, fulls, halves2, fulls2, isem, wsem, ssem, rsem):
    exp, ten = lax.axis_index("exp"), lax.axis_index("ten")
    cx, core = exp // 2, exp % 2
    width = tokens.shape[1]
    half = width // 2
    hidden = wg.shape[2]
    local = wg.shape[0]
    xcut = (width + EXTRA) // 256 * 128 + 128

    def device(axis, d):
        if axis == 0:
            return {"exp": (cx + SIDE + d) % SIDE * 2 + core, "ten": ten}
        return {"exp": exp, "ten": (ten + SIDE + d) % SIDE}

    other = {"exp": cx * 2 + 1 - core, "ten": ten}
    partners = [device(a, d) for a in (0, 1) for d in DIRS] + [other]
    barrier = pltpu.get_barrier_semaphore()
    for p in partners:
        pl.semaphore_signal(barrier, inc=1, device_id=p, device_id_type=MESH)

    small = [pltpu.make_async_copy(a, b, isem.at[i]) for i, (a, b) in enumerate(
        ((tokens_hbm, tokens), (ids_hbm, ids), (prob_hbm, prob), (gain_hbm, gain)))]
    loads = []
    for l in range(local):
        loads.append(pltpu.make_async_copy(wg.at[l], w1.at[l, :, pl.ds(0, hidden)], wsem.at[3 * l]))
        loads.append(pltpu.make_async_copy(wu.at[l], w1.at[l, :, pl.ds(hidden, hidden)], wsem.at[3 * l + 1]))
    for l in range(local):
        loads.append(pltpu.make_async_copy(wd.at[l], w2.at[pl.ds(l * hidden, hidden)], wsem.at[3 * l + 2]))
    for c in small + loads:
        c.start()

    def rows(k, s, dg):
        return pl.ds(((k * 2 + s) * SIDE + dg % SIDE) * ROWS, ROWS)

    def xcols(h):
        return pl.ds(0, xcut) if h == 0 else pl.ds(xcut, width + EXTRA - xcut)

    def ycols(h):
        return pl.ds(h * half, half)

    def xat(df, k, s, dg, h=None):
        if h is None:
            return xbuf.at[df % SIDE, rows(k, s, dg)]
        return xbuf.at[df % SIDE, rows(k, s, dg), xcols(h)]

    def yat(df, k, s, dg, h):
        return ybuf.at[df % SIDE, rows(k, s, dg), ycols(h)]

    def ends(key):
        kind = key[0]
        if kind == "m1":
            _, s, d, h = key
            return xat(0, 0, s, 0, h), xat(-d, 0, s, 0, h), device(axis_of(s, 0), d)
        if kind == "m2":
            _, s, d = key
            return xat(-d, 0, s, 0, fw(d)), xat(2, 0, s, 0, fw(d)), device(axis_of(s, 0), d)
        if kind == "m3":
            _, df, s, d, h = key
            return xat(df, 0, s, 0, h), xat(df, 0, s, -d, h), device(axis_of(s, 1), d)
        if kind == "m4":
            _, df, s, d = key
            return xat(df, 0, s, -d, fw(d)), xat(df, 0, s, 2, fw(d)), device(axis_of(s, 1), d)
        if kind == "m5":
            _, df, s, dg = key
            return xat(df, 0, s, dg), xat(df, 1, s, dg), other
        if kind == "r0":
            _, df, n = key
            part = pl.ds(n * (width // PIECES), width // PIECES)
            return ybuf.at[df, pl.ds(8 * ROWS, 8 * ROWS), part], sib.at[df, :, part], other
        if kind == "r1":
            _, df, s, d = key
            return yat(df, 0, s, 2, fw(d)), halves.at[df, s, fw(d)], device(axis_of(s, 1), d)
        if kind == "r2":
            _, df, s, d, h = key
            return yat(df, 0, s, d, h), fulls.at[df, s, fw(d), :, ycols(h)], device(axis_of(s, 1), d)
        if kind == "r3":
            _, s, d = key
            return yat(2, 0, s, 0, fw(d)), halves2.at[s, fw(d)], device(axis_of(s, 0), d)
        _, s, d, h = key
        return yat(d, 0, s, 0, h), fulls2.at[s, fw(d), :, ycols(h)], device(axis_of(s, 0), d)

    index = {key: i for i, key in enumerate(SENT)}

    def copy(key):
        src, dst, dev = ends(key)
        i = index[key]
        return pltpu.make_async_remote_copy(
            src_ref=src, dst_ref=dst, send_sem=ssem.at[i], recv_sem=rsem.at[i],
            device_id=dev, device_id_type=MESH)

    step = 4 * EXTRA
    count = tokens.shape[0]
    small[0].wait()
    squares = jnp.zeros((count, EXTRA), F32)
    for c in range(0, width, EXTRA):
        piece = tokens[:, c:c + EXTRA].astype(F32)
        squares = squares + piece * piece
    scale = lax.rsqrt(jnp.sum(squares, axis=1, keepdims=True) / width + 1e-06)
    small[3].wait()
    for s in (0, 1):
        scale_s = jnp.broadcast_to(scale[s * ROWS:(s + 1) * ROWS], (ROWS, step))
        for c in range(0, width, step):
            piece = tokens[s * ROWS:(s + 1) * ROWS, c:c + step].astype(F32)
            xbuf[0, rows(0, s, 0), pl.ds(c, step)] = (piece * scale_s * gain[:, c:c + step]).astype(BF16)
    small[1].wait()
    small[2].wait()
    experts = local * SIDE * 2
    mixing = prob[...] / jnp.sum(prob[...], axis=0, keepdims=True)
    chosen = ids[...]
    line = lax.broadcasted_iota(jnp.int32, (2 * experts, count), 0)
    number = jnp.where(line >= experts, line - experts, line)
    mix = jnp.zeros((2 * experts, count), F32)
    for k in range(chosen.shape[0]):
        mine = jnp.broadcast_to(chosen[k:k + 1], line.shape) == number
        mix = mix + jnp.where(mine, jnp.broadcast_to(mixing[k:k + 1], line.shape), 0.0)
    coarse = mix.astype(BF16).astype(F32)
    terms = jnp.where(line >= experts, mix - coarse, coarse).astype(BF16)
    eye = (lax.broadcasted_iota(jnp.int32, (2 * experts, EXTRA), 0)
           == lax.broadcasted_iota(jnp.int32, (2 * experts, EXTRA), 1))
    packed = lax.dot_general(terms, jnp.where(eye, 1.0, 0.0).astype(BF16), (((0,), (0,)), ((), ())),
                             preferred_element_type=F32).astype(BF16)
    for s in (0, 1):
        xbuf[0, rows(0, s, 0), pl.ds(width, EXTRA)] = packed[s * ROWS:(s + 1) * ROWS]
    pl.semaphore_wait(barrier, len(partners))

    lane_line = lax.broadcasted_iota(jnp.int32, (EXTRA, EXTRA), 0)

    def up(df, l):
        both = jnp.dot(xbuf[df, :, pl.ds(0, width)], w1[l], preferred_element_type=F32)
        e = exp * local + l
        pick = jnp.where((lane_line == e) | (lane_line == e + experts), 1.0, 0.0).astype(BF16)
        weight = jnp.dot(xbuf[df, :, pl.ds(width, EXTRA)], pick, preferred_element_type=F32)
        for c in range(0, hidden, EXTRA):
            g, u = both[:, c:c + EXTRA], both[:, hidden + c:hidden + c + EXTRA]
            hid[df, :, pl.ds(l * hidden + c, EXTRA)] = (g / (1.0 + jnp.exp(-g)) * u * weight).astype(BF16)

    def down(df, n):
        part = pl.ds(n * (width // PIECES), width // PIECES)
        ybuf[df, :, part] = jnp.dot(hid[df], w2[:, part], preferred_element_type=F32).astype(BF16)

    def add(df, s, dg, h):
        t = toward(h)
        whole = ybuf[df, rows(0, s, dg), ycols(h)].astype(F32) + sib[df, rows(0, s, dg), ycols(h)].astype(F32)
        if dg == t:
            whole = whole + halves[df, s, h].astype(F32)
        if dg == 0:
            for i in (0, 1):
                whole = whole + fulls[df, s, i, :, ycols(h)].astype(F32)
            if df == 0:
                for i in (0, 1):
                    whole = whole + fulls2[s, i, :, ycols(h)].astype(F32)
                out[pl.ds(s * ROWS, ROWS), ycols(h)] = whole.astype(BF16)
                return
            if df == t % SIDE:
                whole = whole + halves2[s, h].astype(F32)
        ybuf[df, rows(0, s, dg), ycols(h)] = whole.astype(BF16)

    got, loaded = set(), set()

    def load_wait(which):
        for i in which:
            if i not in loaded:
                loaded.add(i)
                loads[i].wait()

    for key in ORDER:
        for m in needs(key):
            if m not in got:
                got.add(m)
                copy(m).wait_recv()
        if key[0] == "U":
            load_wait((2 * key[2], 2 * key[2] + 1))
            up(key[1], key[2])
        elif key[0] == "D":
            load_wait((4, 5))
            down(key[1], key[2])
        elif key[0] == "q":
            add(*key[1:])
        else:
            copy(key).start()
    for m in SENT:
        copy(m).wait_send()


def per_device(tokens, norm_gain, expert_ids, gate_prob, w_gate, w_up, w_down):
    count, width = tokens.shape
    top = expert_ids.shape[1]
    local, _, hidden = w_gate.shape
    hbm = pl.BlockSpec(memory_space=pl.ANY)
    chunk = 2 * 2 * SIDE * ROWS
    return pl.pallas_call(
        kernel,
        out_shape=jax.ShapeDtypeStruct((count, width), BF16),
        in_specs=[hbm] * 7,
        out_specs=pl.BlockSpec(memory_space=pltpu.VMEM),
        scratch_shapes=[
            pltpu.VMEM((count, width), BF16),
            pltpu.VMEM((1, width), F32),
            pltpu.VMEM((top, count), jnp.int32),
            pltpu.VMEM((top, count), F32),
            pltpu.VMEM((SIDE, chunk, width + EXTRA), BF16),
            pltpu.VMEM((local, width, 2 * hidden), BF16),
            pltpu.VMEM((local * hidden, width), BF16),
            pltpu.VMEM((SIDE, chunk, local * hidden), BF16),
            pltpu.VMEM((SIDE, chunk, width), BF16),
            pltpu.VMEM((SIDE, chunk // 2, width), BF16),
            pltpu.VMEM((SIDE, 2, 2, ROWS, width // 2), BF16),
            pltpu.VMEM((SIDE, 2, 2, ROWS, width), BF16),
            pltpu.VMEM((2, 2, ROWS, width // 2), BF16),
            pltpu.VMEM((2, 2, ROWS, width), BF16),
            pltpu.SemaphoreType.DMA((4,)),
            pltpu.SemaphoreType.DMA((3 * local,)),
            pltpu.SemaphoreType.DMA((len(SENT),)),
            pltpu.SemaphoreType.DMA((len(SENT),)),
        ],
        compiler_params=pltpu.CompilerParams(
            collective_id=0, has_side_effects=True, vmem_limit_bytes=60 * 1024 * 1024),
        name="experts",
    )(tokens, norm_gain.reshape(1, width), expert_ids.T, gate_prob.T, w_gate, w_up, w_down)


def solution(mesh):
    placed = (
        P(("grp", "exp", "ten"), None),
        P(),
        P(("grp", "exp", "ten"), None),
        P(("grp", "exp", "ten"), None),
        P("exp", None, "ten"),
        P("exp", None, "ten"),
        P("exp", "ten", None),
    )
    return jax.shard_map(
        per_device,
        mesh=mesh,
        in_specs=placed,
        out_specs=P(("grp", "exp", "ten"), None),
        check_vma=False,
    )
```

time: 201 us -> 76.4 us (0.38)
  waiting for transfers between devices: 99.7 us -> 0 us
  Pallas kernels: 0 us -> 74.5 us
  blocking collectives: 46 us -> 0 us
  matrix products: 36.5 us -> 0 us
  between operations: 13.4 us -> 0.01 us
  other arithmetic: 5.01 us -> 0 us
    reduce_scatter x1 -> x0, waiting for transfers between devices: 92.4 us -> none  [per_device(): lax.psum_scatter(partial.astype(jnp.bfloat16), ('exp', 'ten'), scatter_di...]
    pallas_call x0 -> x1, Pallas kernels: none -> 74.5 us  [per_device(): pl.pallas_call(kernel, out_shape=jax.ShapeDtypeStruct((count, width), BF1...]
    all_gather x1 -> x0, blocking collectives: 46 us -> none  [per_device(): weights = lax.all_gather(weight, ('exp', 'ten'), axis=0, tiled=True)]
    dot_general x2 -> x0, matrix products: 36.5 us -> none  [the longest x1 25.6 us: per_device(): jnp.dot(hidden, w_down.reshape(local_count * hid, width), preferred_eleme...]
    all_gather x1 -> x0, waiting for transfers between devices: 7.25 us -> none  [per_device(): everyone = lax.all_gather(normed, ('exp', 'ten'), axis=0, tiled=True)]
    reduce_sum x3 -> x0, other arithmetic: 2.52 us -> none  [the longest x1 1.11 us: per_device(): meansq = jnp.mean(floats * floats, axis=1, keepdims=True)]
  transfers between devices with their start and end apart: 2 -> 0, of which waited for: 2 -> 0; matrix products, arithmetic and copies ran while one was open for 1% -> 0% of each run, Pallas kernels for 0% -> 0%
where the time goes in v3:
time: 76.4 us; the launch traced here: 76.2 us
  Pallas kernels  74.5 us (98%)
  local copies, waits for them, and re-layouts  1.67 us (2%)
    pallas_call x1, Pallas kernels, per_device(): pl.pallas_call(kernel, out_shape=jax.ShapeDtypeStruct((count, width), BF1...  74.5 us
    unnamed x1, local copies, waits for them, and re-layouts  1.67 us

profile of v3, /device:TPU:0, one launch (start us, length us, event | category | flops | bytes accessed | tf_op | source)
XLA Modules:
  0.0 76.2 jit_solution(15917790599267705658)
XLA Ops:
  0.0 74.5 %experts.1 = bf16[32,4096]{1,0:T(8,128)(2,1)} custom-call(bf16[32,4096]{1,0:T(8,128)(2,1)} %tokens_hbm.1, f32[1,4096]{1,0:T(1,128)} %bitcast.3, s32[8,32]{1,0:T(8,128)} %bitcast.4, f32[8,32]{1,0:T(8,128)} %bitcast.5, bf16[2,4096,384]{2,1,0:T(8,128)(2,1)} %wg.1, bf16[2,4096,384]{2,1,0:T(8,128)(2,1)} %wu.1, bf16[2,384,4096]{2,1,0:T(8,128)(2,1)} %wd.1), custom_call_target="tpu_custom_call" | custom-call | tf_op jit(solution)/shard_map/experts/pallas_call | solution.py:312
  74.5 1.7 %copy.9 = bf16[32,4096]{1,0:T(8,128)(2,1)} copy(bf16[32,4096]{1,0:T(8,128)(2,1)} %experts.1) | data formatting | bytes 524288

commit v4 on v3

--- a/solution.py
+++ b/solution.py
@@ -15,50 +15,49 @@
 PIECES = 4
 DIRS = (1, -1)
 ORDER = (
-    ("m3", 0, 1, 1, 0), ("m1", 0, 1, 0), ("m1", 0, 1, 1), ("m1", 1, 1, 1), ("m3", 0, 1, -1, 1), ("m3", 0, 0, 1, 0),
-    ("m1", 1, 1, 0), ("m5", 0, 0, 0), ("m3", 0, 1, 1, 1), ("m3", 0, 0, -1, 1), ("m5", 0, 1, 0), ("m3", 0, 1, -1, 0),
-    ("m1", 1, -1, 1), ("m1", 0, -1, 1), ("m3", 0, 0, -1, 0), ("m3", 0, 0, 1, 1), ("m4", 0, 0, -1), ("m5", 0, 1, 1),
-    ("m4", 0, 1, -1), ("m4", 0, 1, 1), ("m3", 3, 0, -1, 1), ("m4", 0, 0, 1), ("m3", 3, 0, -1, 0), ("m3", 3, 1, 1, 0),
-    ("m3", 3, 1, -1, 1), ("m3", 3, 1, -1, 0), ("m2", 1, -1), ("m2", 0, -1), ("m3", 3, 0, 1, 0), ("m5", 0, 0, 1),
-    ("m1", 0, -1, 0), ("m2", 1, 1), ("m5", 3, 0, 0), ("m3", 3, 0, 1, 1), ("m2", 0, 1), ("m5", 0, 0, 3),
-    ("m5", 0, 1, 3), ("m5", 0, 1, 2), ("m4", 3, 0, -1), ("m1", 1, -1, 0), ("m3", 3, 1, 1, 1), ("m5", 0, 0, 2),
-    ("m4", 3, 1, 1), ("m4", 3, 0, 1), ("m4", 3, 1, -1), ("m5", 3, 0, 1), ("U", 0, 0), ("m5", 2, 0, 0),
-    ("m3", 2, 0, -1, 1), ("m3", 2, 1, -1, 1), ("m3", 1, 1, -1, 1), ("m5", 2, 1, 0), ("m5", 3, 1, 1),
-    ("m3", 2, 1, -1, 0), ("m3", 2, 0, 1, 0), ("m3", 2, 0, 1, 1), ("m5", 3, 1, 0), ("m3", 2, 1, 1, 1),
-    ("m3", 2, 0, -1, 0), ("m3", 1, 0, -1, 1), ("m3", 2, 1, 1, 0), ("m5", 3, 1, 3), ("U", 0, 1), ("m5", 3, 0, 2),
-    ("m3", 1, 1, 1, 1), ("m5", 3, 0, 3), ("m5", 3, 1, 2), ("D", 0, 0), ("D", 0, 3), ("r0", 0, 0), ("m3", 1, 1, 1, 0),
-    ("r0", 0, 3), ("D", 0, 1), ("r0", 0, 1), ("m4", 2, 0, 1), ("D", 0, 2), ("r0", 0, 2), ("m5", 1, 0, 0),
-    ("m3", 1, 0, 1, 1), ("m3", 1, 0, 1, 0), ("m4", 2, 1, -1), ("m4", 2, 0, -1), ("m4", 2, 1, 1), ("U", 3, 1),
-    ("m5", 2, 0, 1), ("m5", 2, 1, 3), ("U", 3, 0), ("m5", 2, 0, 3), ("q", 0, 1, 2, 0), ("r1", 0, 1, 1),
-    ("m5", 1, 1, 0), ("m3", 1, 1, -1, 0), ("D", 3, 3), ("q", 0, 1, -1, 0), ("m5", 2, 0, 2), ("m4", 1, 0, -1),
-    ("q", 0, 1, 2, 1), ("m5", 2, 1, 2), ("m5", 2, 1, 1), ("m3", 1, 0, -1, 0), ("q", 0, 0, -1, 0), ("q", 0, 0, 2, 1),
-    ("D", 3, 2), ("q", 0, 1, 1, 1), ("r0", 3, 2), ("r1", 0, 1, -1), ("D", 3, 1), ("r0", 3, 1), ("m4", 1, 1, 1),
-    ("m4", 1, 0, 1), ("q", 0, 0, 1, 1), ("D", 3, 0), ("r0", 3, 3), ("q", 0, 1, 1, 0), ("r2", 0, 1, 1, 1),
-    ("r2", 0, 1, -1, 0), ("r2", 0, 1, 1, 0), ("m5", 1, 1, 1), ("q", 0, 0, 2, 0), ("r1", 0, 0, 1), ("m4", 1, 1, -1),
-    ("U", 2, 0), ("r0", 3, 0), ("U", 2, 1), ("m5", 1, 0, 3), ("q", 3, 0, 2, 1), ("r1", 3, 0, -1), ("m5", 1, 0, 1),
-    ("q", 0, 1, -1, 1), ("q", 3, 1, 1, 1), ("m5", 1, 1, 3), ("D", 2, 1), ("m5", 1, 0, 2), ("q", 3, 1, 2, 0),
-    ("r2", 0, 0, 1, 1), ("q", 3, 0, -1, 0), ("r2", 3, 0, -1, 0), ("r2", 0, 1, -1, 1), ("r2", 0, 0, -1, 0),
-    ("q", 3, 0, 1, 1), ("m5", 1, 1, 2), ("q", 3, 0, 2, 0), ("r1", 3, 0, 1), ("r1", 3, 1, 1), ("r0", 2, 1),
-    ("q", 3, 1, -1, 0), ("D", 2, 2), ("r2", 3, 1, -1, 0), ("D", 2, 0), ("r2", 3, 1, 1, 1), ("r2", 3, 0, 1, 1),
-    ("r0", 2, 0), ("D", 2, 3), ("r0", 2, 3), ("r1", 0, 0, -1), ("r0", 2, 2), ("U", 1, 1), ("q", 2, 1, 2, 0),
-    ("r1", 2, 1, 1), ("q", 2, 1, -1, 0), ("r2", 2, 1, -1, 0), ("q", 2, 0, 2, 0), ("r1", 2, 0, 1), ("q", 3, 0, 1, 0),
-    ("r2", 3, 0, 1, 0), ("q", 3, 0, -1, 1), ("r2", 3, 0, -1, 1), ("q", 3, 1, 2, 1), ("r1", 3, 1, -1), ("U", 1, 0),
-    ("D", 1, 3), ("r0", 1, 3), ("q", 2, 0, 2, 1), ("r1", 2, 0, -1), ("q", 2, 1, 2, 1), ("r1", 2, 1, -1), ("D", 1, 2),
-    ("r0", 1, 2), ("q", 2, 0, 1, 1), ("r2", 2, 0, 1, 1), ("q", 3, 1, 1, 0), ("r2", 3, 1, 1, 0), ("q", 2, 0, -1, 0),
-    ("r2", 2, 0, -1, 0), ("D", 1, 1), ("q", 2, 1, 1, 0), ("r0", 1, 1), ("q", 3, 1, -1, 1), ("r2", 3, 1, -1, 1),
-    ("q", 2, 0, 1, 0), ("r2", 2, 1, 1, 0), ("r2", 2, 0, 1, 0), ("D", 1, 0), ("r0", 1, 0), ("q", 1, 0, 2, 1),
-    ("r1", 1, 0, -1), ("q", 2, 0, -1, 1), ("r2", 2, 0, -1, 1), ("q", 1, 1, 2, 1), ("r1", 1, 1, -1),
-    ("q", 1, 0, 1, 1), ("r2", 1, 0, 1, 1), ("q", 2, 1, 1, 1), ("q", 2, 1, -1, 1), ("r2", 2, 1, 1, 1),
-    ("r2", 2, 1, -1, 1), ("q", 1, 0, -1, 0), ("r2", 1, 0, -1, 0), ("q", 1, 1, 2, 0), ("r1", 1, 1, 1),
-    ("q", 1, 0, 2, 0), ("r1", 1, 0, 1), ("q", 2, 0, 0, 0), ("q", 2, 1, 0, 0), ("q", 1, 0, -1, 1), ("r3", 1, 1),
-    ("r2", 1, 0, -1, 1), ("q", 0, 0, -1, 1), ("q", 1, 1, -1, 1), ("r2", 1, 1, -1, 1), ("r3", 0, 1),
-    ("q", 1, 1, -1, 0), ("q", 2, 0, 0, 1), ("r3", 0, -1), ("q", 1, 1, 1, 1), ("r2", 1, 1, 1, 1), ("q", 2, 1, 0, 1),
-    ("r3", 1, -1), ("r2", 1, 1, -1, 0), ("r2", 0, 0, -1, 1), ("q", 1, 1, 1, 0), ("q", 1, 0, 1, 0),
-    ("r2", 1, 0, 1, 0), ("q", 0, 0, 1, 0), ("r2", 0, 0, 1, 0), ("q", 3, 1, 0, 0), ("q", 3, 0, 0, 0),
-    ("r2", 1, 1, 1, 0), ("r4", 0, -1, 0), ("r4", 1, -1, 0), ("q", 1, 0, 0, 1), ("r4", 0, 1, 1), ("q", 1, 1, 0, 1),
-    ("r4", 1, 1, 1), ("q", 3, 1, 0, 1), ("q", 3, 0, 0, 1), ("r4", 1, -1, 1), ("q", 1, 0, 0, 0), ("r4", 0, -1, 1),
-    ("r4", 0, 1, 0), ("q", 1, 1, 0, 0), ("r4", 1, 1, 0), ("q", 0, 0, 0, 1), ("q", 0, 0, 0, 0), ("q", 0, 1, 0, 1),
-    ("q", 0, 1, 0, 0),
+    ("m1", 0, -1, 0), ("m3", 0, 1, 1, 0), ("m3", 0, 0, 1, 0), ("m3", 0, 0, -1, 1), ("m1", 1, -1, 1), ("m1", 0, 1, 0),
+    ("m1", 1, 1, 0), ("m1", 1, -1, 0), ("m5", 0, 0, 0), ("m3", 0, 1, -1, 1), ("m1", 0, -1, 1), ("m3", 0, 1, 1, 1),
+    ("m3", 0, 1, -1, 0), ("m3", 0, 0, 1, 1), ("m4", 0, 1, 1), ("m4", 0, 0, 1), ("m4", 0, 0, -1), ("m3", 1, 0, 1, 0),
+    ("m1", 0, 1, 1), ("m3", 0, 0, -1, 0), ("m4", 0, 1, -1), ("m3", 1, 1, -1, 1), ("m3", 1, 1, 1, 0), ("m5", 1, 1, 0),
+    ("m5", 0, 1, 0), ("m3", 1, 0, -1, 1), ("m5", 1, 0, 0), ("m2", 1, 1), ("m2", 0, -1), ("m2", 0, 1),
+    ("m5", 0, 0, 3), ("m3", 1, 1, -1, 0), ("m3", 1, 1, 1, 1), ("m2", 1, -1), ("m3", 1, 0, 1, 1), ("m5", 0, 1, 3),
+    ("m1", 1, 1, 1), ("m5", 0, 1, 1), ("m5", 0, 0, 2), ("m5", 0, 1, 2), ("m5", 0, 0, 1), ("m3", 1, 0, -1, 0),
+    ("m4", 1, 0, -1), ("m5", 3, 0, 0), ("m4", 1, 1, 1), ("m3", 2, 1, 1, 0), ("m4", 1, 0, 1), ("m3", 3, 1, 1, 0),
+    ("m4", 1, 1, -1), ("m3", 3, 0, 1, 0), ("m3", 2, 1, -1, 0), ("U", 0, 1), ("m3", 2, 1, -1, 1), ("m5", 2, 0, 0),
+    ("m5", 1, 0, 3), ("m3", 2, 0, 1, 0), ("m3", 2, 0, -1, 1), ("m5", 2, 1, 0), ("m5", 1, 1, 3), ("m5", 1, 1, 1),
+    ("m3", 2, 0, -1, 0), ("m3", 3, 0, -1, 1), ("m5", 1, 0, 1), ("U", 0, 0), ("m3", 2, 0, 1, 1), ("m5", 1, 0, 2),
+    ("m5", 1, 1, 2), ("D", 0, 1), ("m3", 3, 1, -1, 1), ("m5", 3, 1, 0), ("m3", 3, 1, -1, 0), ("m3", 3, 1, 1, 1),
+    ("D", 0, 2), ("r0", 0, 1), ("r0", 0, 2), ("D", 0, 3), ("r0", 0, 3), ("D", 0, 0), ("m4", 2, 0, -1),
+    ("m4", 2, 1, -1), ("m3", 2, 1, 1, 1), ("m5", 2, 1, 1), ("m4", 2, 1, 1), ("m3", 3, 0, -1, 0), ("r0", 0, 0),
+    ("m4", 2, 0, 1), ("U", 1, 0), ("m5", 2, 0, 3), ("m5", 2, 0, 1), ("q", 0, 1, 1, 1), ("r2", 0, 1, 1, 1),
+    ("m4", 3, 0, -1), ("m4", 3, 0, 1), ("U", 1, 1), ("q", 0, 0, 1, 1), ("q", 0, 1, 2, 0), ("q", 0, 1, -1, 0),
+    ("r2", 0, 1, -1, 0), ("r2", 0, 0, 1, 1), ("m5", 2, 1, 3), ("q", 0, 0, 2, 0), ("m5", 2, 0, 2), ("m3", 3, 0, 1, 1),
+    ("m5", 3, 1, 3), ("q", 0, 0, 2, 1), ("r1", 0, 0, -1), ("D", 1, 0), ("m5", 2, 1, 2), ("r1", 0, 0, 1), ("D", 1, 2),
+    ("D", 1, 1), ("m4", 3, 1, 1), ("r0", 1, 1), ("r0", 1, 0), ("r0", 1, 2), ("m4", 3, 1, -1), ("D", 1, 3),
+    ("r0", 1, 3), ("m5", 3, 1, 1), ("m5", 3, 0, 1), ("m5", 3, 0, 2), ("U", 2, 1), ("U", 2, 0), ("m5", 3, 0, 3),
+    ("m5", 3, 1, 2), ("q", 1, 1, 2, 1), ("D", 2, 3), ("r0", 2, 3), ("r1", 1, 1, -1), ("q", 1, 0, -1, 0),
+    ("r2", 1, 0, -1, 0), ("D", 2, 1), ("r0", 2, 1), ("D", 2, 2), ("r0", 2, 2), ("D", 2, 0), ("r0", 2, 0),
+    ("q", 1, 0, 2, 1), ("q", 1, 1, -1, 0), ("r1", 0, 1, 1), ("r1", 1, 0, -1), ("q", 1, 0, 2, 0), ("U", 3, 1),
+    ("q", 2, 0, 2, 0), ("r1", 2, 0, 1), ("r2", 1, 1, -1, 0), ("r1", 1, 0, 1), ("q", 1, 1, 2, 0), ("r1", 1, 1, 1),
+    ("q", 2, 0, -1, 0), ("r2", 2, 0, -1, 0), ("q", 2, 1, 2, 0), ("r1", 2, 1, 1), ("q", 2, 0, 2, 1),
+    ("q", 2, 0, 1, 1), ("r2", 2, 0, 1, 1), ("q", 2, 1, 2, 1), ("r1", 2, 0, -1), ("r1", 2, 1, -1), ("q", 2, 1, -1, 0),
+    ("r2", 2, 1, -1, 0), ("q", 0, 1, 2, 1), ("q", 2, 1, 1, 1), ("U", 3, 0), ("r2", 2, 1, 1, 1), ("D", 3, 1),
+    ("r0", 3, 1), ("q", 1, 0, -1, 1), ("r1", 0, 1, -1), ("r2", 1, 0, -1, 1), ("D", 3, 0), ("r0", 3, 0),
+    ("q", 2, 0, 1, 0), ("r2", 2, 0, 1, 0), ("q", 1, 1, 1, 1), ("r2", 1, 1, 1, 1), ("D", 3, 3), ("r0", 3, 3),
+    ("q", 2, 1, 1, 0), ("r2", 2, 1, 1, 0), ("q", 1, 0, 1, 1), ("r2", 1, 0, 1, 1), ("q", 2, 1, -1, 1),
+    ("r2", 2, 1, -1, 1), ("q", 2, 0, -1, 1), ("r2", 2, 0, -1, 1), ("D", 3, 2), ("r0", 3, 2), ("q", 3, 0, 2, 0),
+    ("r1", 3, 0, 1), ("q", 0, 0, -1, 0), ("r2", 0, 0, -1, 0), ("q", 3, 1, 2, 0), ("r1", 3, 1, 1), ("q", 1, 1, -1, 1),
+    ("q", 0, 0, 1, 0), ("r2", 1, 1, -1, 1), ("q", 2, 0, 0, 0), ("r3", 0, 1), ("q", 1, 0, 1, 0), ("r2", 1, 0, 1, 0),
+    ("q", 3, 0, 2, 1), ("r1", 3, 0, -1), ("q", 3, 1, 2, 1), ("r1", 3, 1, -1), ("q", 3, 0, 1, 1), ("r2", 3, 0, 1, 1),
+    ("q", 3, 0, -1, 0), ("q", 3, 1, 1, 1), ("q", 3, 1, -1, 0), ("r2", 3, 1, -1, 0), ("r2", 3, 1, 1, 1),
+    ("q", 2, 1, 0, 1), ("r2", 3, 0, -1, 0), ("q", 0, 1, 1, 0), ("q", 2, 0, 0, 1), ("r3", 0, -1), ("q", 3, 1, 1, 0),
+    ("r2", 3, 1, 1, 0), ("r3", 1, -1), ("q", 3, 0, 1, 0), ("r2", 3, 0, 1, 0), ("q", 2, 1, 0, 0), ("r3", 1, 1),
+    ("r2", 0, 0, 1, 0), ("q", 1, 1, 1, 0), ("r2", 1, 1, 1, 0), ("q", 3, 0, -1, 1), ("r2", 3, 0, -1, 1),
+    ("q", 3, 1, -1, 1), ("r2", 3, 1, -1, 1), ("q", 1, 0, 0, 1), ("r4", 0, 1, 1), ("q", 0, 1, -1, 1),
+    ("r2", 0, 1, -1, 1), ("q", 0, 0, -1, 1), ("r2", 0, 0, -1, 1), ("q", 1, 0, 0, 0), ("q", 3, 1, 0, 0),
+    ("q", 3, 0, 0, 0), ("r4", 0, -1, 0), ("q", 1, 1, 0, 1), ("r4", 1, -1, 0), ("r4", 1, 1, 1), ("r4", 0, 1, 0),
+    ("r2", 0, 1, 1, 0), ("q", 3, 0, 0, 1), ("r4", 0, -1, 1), ("q", 3, 1, 0, 1), ("r4", 1, -1, 1), ("q", 1, 1, 0, 0),
+    ("r4", 1, 1, 0), ("q", 0, 0, 0, 0), ("q", 0, 0, 0, 1), ("q", 0, 1, 0, 1), ("q", 0, 1, 0, 0),
 )
 SENT = tuple(k for k in ORDER if k[0] not in ("U", "D", "q"))
 
@@ -118,8 +117,8 @@
     return []
 
 
-def kernel(tokens_hbm, gain_hbm, ids_hbm, prob_hbm, wg, wu, wd, out, tokens, gain, ids, prob,
-           xbuf, w1, w2, hid, ybuf, sib, halves, fulls, halves2, fulls2, isem, wsem, ssem, rsem):
+def kernel(tokens_hbm, gain_hbm, ids_hbm, prob_hbm, wg, wu, wd, out_hbm, tokens, gain, ids, prob, out,
+           xbuf, w1, w2, hid, ybuf, sib, halves, fulls, halves2, fulls2, isem, osem, wsem, ssem, rsem):
     exp, ten = lax.axis_index("exp"), lax.axis_index("ten")
     cx, core = exp // 2, exp % 2
     width = tokens.shape[1]
@@ -147,7 +146,7 @@
         loads.append(pltpu.make_async_copy(wu.at[l], w1.at[l, :, pl.ds(hidden, hidden)], wsem.at[3 * l + 1]))
     for l in range(local):
         loads.append(pltpu.make_async_copy(wd.at[l], w2.at[pl.ds(l * hidden, hidden)], wsem.at[3 * l + 2]))
-    for c in small + loads:
+    for c in small:
         c.start()
 
     def rows(k, s, dg):
@@ -209,20 +208,7 @@
             src_ref=src, dst_ref=dst, send_sem=ssem.at[i], recv_sem=rsem.at[i],
             device_id=dev, device_id_type=MESH)
 
-    step = 4 * EXTRA
     count = tokens.shape[0]
-    small[0].wait()
-    squares = jnp.zeros((count, EXTRA), F32)
-    for c in range(0, width, EXTRA):
-        piece = tokens[:, c:c + EXTRA].astype(F32)
-        squares = squares + piece * piece
-    scale = lax.rsqrt(jnp.sum(squares, axis=1, keepdims=True) / width + 1e-06)
-    small[3].wait()
-    for s in (0, 1):
-        scale_s = jnp.broadcast_to(scale[s * ROWS:(s + 1) * ROWS], (ROWS, step))
-        for c in range(0, width, step):
-            piece = tokens[s * ROWS:(s + 1) * ROWS, c:c + step].astype(F32)
-            xbuf[0, rows(0, s, 0), pl.ds(c, step)] = (piece * scale_s * gain[:, c:c + step]).astype(BF16)
     small[1].wait()
     small[2].wait()
     experts = local * SIDE * 2
@@ -242,6 +228,19 @@
                              preferred_element_type=F32).astype(BF16)
     for s in (0, 1):
         xbuf[0, rows(0, s, 0), pl.ds(width, EXTRA)] = packed[s * ROWS:(s + 1) * ROWS]
+    step = 4 * EXTRA
+    small[0].wait()
+    squares = jnp.zeros((count, EXTRA), F32)
+    for c in range(0, width, EXTRA):
+        piece = tokens[:, c:c + EXTRA].astype(F32)
+        squares = squares + piece * piece
+    scale = lax.rsqrt(jnp.sum(squares, axis=1, keepdims=True) / width + 1e-06)
+    small[3].wait()
+    for s in (0, 1):
+        scale_s = jnp.broadcast_to(scale[s * ROWS:(s + 1) * ROWS], (ROWS, step))
+        for c in range(0, width, step):
+            piece = tokens[s * ROWS:(s + 1) * ROWS, c:c + step].astype(F32)
+            xbuf[0, rows(0, s, 0), pl.ds(c, step)] = (piece * scale_s * gain[:, c:c + step]).astype(BF16)
     pl.semaphore_wait(barrier, len(partners))
 
     lane_line = lax.broadcasted_iota(jnp.int32, (EXTRA, EXTRA), 0)
@@ -271,11 +270,15 @@
                 for i in (0, 1):
                     whole = whole + fulls2[s, i, :, ycols(h)].astype(F32)
                 out[pl.ds(s * ROWS, ROWS), ycols(h)] = whole.astype(BF16)
+                place = pl.ds(s * ROWS, ROWS), ycols(h)
+                results.append(pltpu.make_async_copy(out.at[place], out_hbm.at[place], osem.at[2 * s + h]))
+                results[-1].start()
                 return
             if df == t % SIDE:
                 whole = whole + halves2[s, h].astype(F32)
         ybuf[df, rows(0, s, dg), ycols(h)] = whole.astype(BF16)
 
+    results = []
     got, loaded = set(), set()
 
     def load_wait(which):
@@ -285,6 +288,9 @@
                 loads[i].wait()
 
     for key in ORDER:
+        if needs(key) and not got:
+            for c in loads:
+                c.start()
         for m in needs(key):
             if m not in got:
                 got.add(m)
@@ -301,6 +307,8 @@
             copy(key).start()
     for m in SENT:
         copy(m).wait_send()
+    for c in results:
+        c.wait()
 
 
 def per_device(tokens, norm_gain, expert_ids, gate_prob, w_gate, w_up, w_down):
@@ -313,12 +321,13 @@
         kernel,
         out_shape=jax.ShapeDtypeStruct((count, width), BF16),
         in_specs=[hbm] * 7,
-        out_specs=pl.BlockSpec(memory_space=pltpu.VMEM),
+        out_specs=hbm,
         scratch_shapes=[
             pltpu.VMEM((count, width), BF16),
             pltpu.VMEM((1, width), F32),
             pltpu.VMEM((top, count), jnp.int32),
             pltpu.VMEM((top, count), F32),
+            pltpu.VMEM((count, width), BF16),
             pltpu.VMEM((SIDE, chunk, width + EXTRA), BF16),
             pltpu.VMEM((local, width, 2 * hidden), BF16),
             pltpu.VMEM((local * hidden, width), BF16),
@@ -329,6 +338,7 @@
             pltpu.VMEM((SIDE, 2, 2, ROWS, width), BF16),
             pltpu.VMEM((2, 2, ROWS, width // 2), BF16),
             pltpu.VMEM((2, 2, ROWS, width), BF16),
+            pltpu.SemaphoreType.DMA((4,)),
             pltpu.SemaphoreType.DMA((4,)),
             pltpu.SemaphoreType.DMA((3 * local,)),
             pltpu.SemaphoreType.DMA((len(SENT),)),

time: 76.4 us -> 65.8 us (0.86)
  Pallas kernels: 74.5 us -> 63.9 us
    pallas_call x1, Pallas kernels: 74.5 us -> 63.9 us  [per_device(): pl.pallas_call(kernel, out_shape=jax.ShapeDtypeStruct((count, width), BF1...]
where the time goes in v4:
time: 65.8 us; the launch traced here: 65.6 us
  Pallas kernels  63.9 us (97%)
  local copies, waits for them, and re-layouts  1.67 us (3%)
    pallas_call x1, Pallas kernels, per_device(): pl.pallas_call(kernel, out_shape=jax.ShapeDtypeStruct((count, width), BF1...  63.9 us
    unnamed x1, local copies, waits for them, and re-layouts  1.67 us

profile of v4, /device:TPU:0, one launch (start us, length us, event | category | flops | bytes accessed | tf_op | source)
XLA Modules:
  0.0 65.6 jit_solution(1229701087281900251)
XLA Ops:
  0.0 63.9 %experts.1 = bf16[32,4096]{1,0:T(8,128)(2,1)} custom-call(bf16[32,4096]{1,0:T(8,128)(2,1)} %tokens_hbm.1, f32[1,4096]{1,0:T(1,128)} %bitcast.3, s32[8,32]{1,0:T(8,128)} %bitcast.4, f32[8,32]{1,0:T(8,128)} %bitcast.5, bf16[2,4096,384]{2,1,0:T(8,128)(2,1)} %wg.1, bf16[2,4096,384]{2,1,0:T(8,128)(2,1)} %wu.1, bf16[2,384,4096]{2,1,0:T(8,128)(2,1)} %wd.1), custom_call_target="tpu_custom_call" | custom-call | tf_op jit(solution)/shard_map/experts/pallas_call | solution.py:320
  63.9 1.7 %copy.9 = bf16[32,4096]{1,0:T(8,128)(2,1)} copy(bf16[32,4096]{1,0:T(8,128)(2,1)} %experts.1) | data formatting | bytes 524288
